TPU v7x, 256 devices: a whole 4x4x8 slice. The times are simulated.
256 devices in a mesh: tile: 32 (over x_lo, z, core), head: 8 (over y, x_hi).
Axes of the slice: x: 4 (x_hi: 2, x_lo: 2; x = x_hi * 2 + x_lo), y: 4, z: 8, core: 2. Of those that a mesh axis runs over, the one named last changes fastest.
Arguments:
- attn_proj: bfloat16 [32, 3, 192, 3, 3072], P('tile', None, 'head')
- mlp_proj: bfloat16 [32, 3, 192, 6144], P('tile', None, 'head'), may hold values from -6 to 6
- stream: bfloat16 [32, 3, 192, 3072], P('tile', None, 'head'), may hold values from -6 to 6
- text_len: int32 [32], P('tile'), may hold values from 1 to 192, as said below
- q_gain: float32 [128], replicated
- k_gain: float32 [128], replicated
- w_out_attn: bfloat16 [3072, 3072], P('head', 'tile'), may hold values from -0.0625 to 0.0625
- w_out_mlp: bfloat16 [6144, 3072], P('head', 'tile'), may hold values from -0.0625 to 0.0625
- bias_out: float32 [3072], replicated, may hold values from -3 to 3
- gate_mod: float32 [32, 3072], P('tile'), may hold values from -4 to 4
- final_shift: float32 [32, 3072], P('tile'), may hold values from -3 to 3
- final_scale: float32 [32, 3072], P('tile'), may hold values from -3 to 3
- w_final: bfloat16 [3072, 64], replicated, may hold values from -0.109375 to 0.109375
- b_final: float32 [64], replicated, may hold values from -3 to 3
- latent: float32 [32, 2, 192, 64], P('tile', None, 'head'), may hold values from -6 to 6
- step_size: float32 [32], P('tile'), may hold values from -0.4 to -0.1
Outputs:
- hidden_out: bfloat16 [32, 3, 192, 3072], P('tile', None, 'head')
- latent_next: float32 [32, 2, 192, 64], P('tile', None, 'head')
Inputs may be any that keep to these rules, and one draw needn't show every extreme that they name: `text_len`: live text slots of each request; some request has all 192 text slots live in every draw.
All inputs are finite; a program needn't handle non-finite values.
Results may differ from a plain program's by a relative error of at most 0.0098.
Values may be sent and summed in bfloat16 or wider, within the bound.
A program may use at most 128 MiB of HBM per device.

v0:
```python
import functools
import math

import jax
import jax.numpy as jnp
import numpy as np
from jax import lax
from jax.experimental import pallas as pl
from jax.experimental.pallas import tpu as pltpu
from jax.sharding import PartitionSpec as P

HEAD_DIM = 128
SLOTS = 192
GRID_W = 32
MESH = pl.DeviceIdType.MESH
F32 = jnp.float32
BF16 = jnp.bfloat16


def rope_constants(groups):
    zero = HEAD_DIM // 16
    axis = (HEAD_DIM // 2 - zero) // 2
    own = SLOTS // groups
    freqs = (10000.0 ** (-np.arange(axis, dtype=np.float32) / np.float32(axis))).astype(np.float32)
    angles = np.zeros((3, SLOTS, HEAD_DIM // 2), np.float32)
    for block in (1, 2):
        index = (block - 1) * SLOTS + np.arange(SLOTS)
        angles[block, :, zero : zero + axis] = (index // GRID_W).astype(np.float32)[:, None] * freqs
        angles[block, :, zero + axis :] = (index % GRID_W).astype(np.float32)[:, None] * freqs
    order = angles.reshape(3, groups, own, HEAD_DIM // 2).transpose(1, 0, 2, 3)
    wide = np.repeat(order.astype(np.float64), 2, axis=-1)
    sign = np.where(np.arange(HEAD_DIM) % 2 == 0, -1.0, 1.0)
    cosine = np.cos(wide).astype(np.float32)
    sine = (np.sin(wide) * sign).astype(np.float32)
    slot = np.full((3, SLOTS), -1, np.int32)
    slot[0] = np.arange(SLOTS)
    slot = slot.reshape(3, groups, own).transpose(1, 0, 2).reshape(1, -1)
    return cosine, sine, slot


def swap_pairs(x, even):
    return jnp.where(even, pltpu.roll(x, HEAD_DIM - 1, axis=x.ndim - 1), pltpu.roll(x, 1, axis=x.ndim - 1))


def layer_kernel(
    cfg,
    text_len,
    step_size,
    attn_in,
    mlp_in,
    stream_in,
    weight_attn,
    weight_mlp,
    w_final,
    cosine,
    sine,
    slot_number,
    q_gain,
    k_gain,
    bias_out,
    gate,
    shift,
    scale,
    b_final,
    latent,
    hidden_out,
    latent_out,
    got_attn,
    got_mlp,
    weights,
    queries,
    keys,
    values,
    mlp_act,
    act,
    product,
    outgoing,
    incoming,
    mine,
    updated,
    stream,
    final_w,
    table_c,
    table_s,
    local_sem,
    attn_send,
    attn_recv,
    mlp_send,
    mlp_recv,
    ring_send,
    ring_recv,
    side_send,
    side_recv,
    part_send,
    part_recv,
):
    heads_n, z_n, chunks, own_rows, own_slots = cfg
    tile = lax.axis_index("tile")
    head = lax.axis_index("head")
    core = tile % 2
    depth = (tile // 2) % z_n
    half = tile // (2 * z_n)
    width = got_attn.shape[4]
    units = got_mlp.shape[3]
    local_heads = width // HEAD_DIM
    shard = weights.shape[1]
    per_chunk = weights.shape[0] // chunks
    columns = shard * per_chunk
    rows = heads_n * own_rows

    def tile_at(half_, depth_, core_):
        return half_ * (2 * z_n) + depth_ * 2 + core_

    up = tile_at(half, (depth + 1) % z_n, core)
    down = tile_at(half, (depth + z_n - 1) % z_n, core)
    across = tile_at(1 - half, depth, core)
    sibling = tile_at(half, depth, 1 - core)

    def local_copies():
        at = pl.ds(pl.multiple_of(head * width, width), width)
        mt = pl.ds(pl.multiple_of(head * units, units), units)
        return [
            pltpu.make_async_copy(attn_in.at[:, :, :, at], got_attn.at[head], local_sem.at[0]),
            pltpu.make_async_copy(mlp_in.at[:, :, mt], got_mlp.at[head], local_sem.at[1]),
            pltpu.make_async_copy(weight_attn, weights.at[tile, :, pl.ds(0, width)], local_sem.at[2]),
            pltpu.make_async_copy(weight_mlp, weights.at[tile, :, pl.ds(width, units)], local_sem.at[3]),
            pltpu.make_async_copy(stream_in, stream, local_sem.at[4]),
            pltpu.make_async_copy(w_final, final_w, local_sem.at[5]),
        ]

    for copy in local_copies():
        copy.start()

    barrier = pltpu.get_barrier_semaphore()
    for neighbour in (up, down, across, sibling):
        pl.semaphore_signal(barrier, inc=1, device_id={"tile": neighbour}, device_id_type=MESH)

    def greet(i, _):
        pl.semaphore_signal(barrier, inc=1, device_id={"head": (head + i) % heads_n}, device_id_type=MESH)
        return 0

    lax.fori_loop(1, heads_n, greet, 0)
    pl.semaphore_wait(barrier, heads_n - 1 + 4)

    def attn_copy(i, peer, source):
        return pltpu.make_async_remote_copy(
            src_ref=attn_in.at[:, :, :, pl.ds(pl.multiple_of(peer * width, width), width)],
            dst_ref=got_attn.at[source],
            send_sem=attn_send.at[i],
            recv_sem=attn_recv.at[i],
            device_id={"head": peer},
            device_id_type=MESH,
        )

    def mlp_copy(i, peer, source):
        return pltpu.make_async_remote_copy(
            src_ref=mlp_in.at[:, :, pl.ds(pl.multiple_of(peer * units, units), units)],
            dst_ref=got_mlp.at[source],
            send_sem=mlp_send.at[i],
            recv_sem=mlp_recv.at[i],
            device_id={"head": peer},
            device_id_type=MESH,
        )

    def send_attn(i, _):
        attn_copy(i, (head + i) % heads_n, head).start()
        return 0

    def send_mlp(i, _):
        mlp_copy(i, (head + i) % heads_n, head).start()
        return 0

    lax.fori_loop(1, heads_n, send_attn, 0)

    def ring_copy(stream_, direction, step, slot):
        return pltpu.make_async_remote_copy(
            src_ref=weights.at[slot],
            dst_ref=weights.at[slot],
            send_sem=ring_send.at[stream_, direction, step],
            recv_sem=ring_recv.at[stream_, direction, step],
            device_id={"tile": up if direction == 0 else down},
            device_id_type=MESH,
        )

    def side_copy(index, slot, to):
        return pltpu.make_async_remote_copy(
            src_ref=weights.at[slot],
            dst_ref=weights.at[slot],
            send_sem=side_send.at[index],
            recv_sem=side_recv.at[index],
            device_id={"tile": to},
            device_id_type=MESH,
        )

    reach = (z_n // 2, z_n - 1 - z_n // 2)

    def half_of(stream_):
        return half if stream_ == 0 else 1 - half

    def arrival(stream_, direction, step):
        offset = z_n - step if direction == 0 else step
        slot = tile_at(half_of(stream_), (depth + offset) % z_n, core)
        return slot, stream_ * z_n + (offset if offset < z_n else 0)

    def begin(stream_):
        slot = tile_at(half_of(stream_), depth, core)
        ring_copy(stream_, 0, 1, slot).start()
        ring_copy(stream_, 1, 1, slot).start()
        side_copy(stream_ * z_n, slot, sibling).start()

    def advance(stream_, step):
        for direction in (0, 1):
            if step <= reach[direction]:
                slot, number = arrival(stream_, direction, step)
                ring_copy(stream_, direction, step, slot).wait_recv()
                if step < reach[direction]:
                    ring_copy(stream_, direction, step + 1, slot).start()
                side_copy(number, slot, sibling).start()

    cross = 2 * z_n
    locals_ = local_copies()
    locals_[2].wait()
    locals_[3].wait()
    side_copy(cross, tile, across).start()
    begin(0)
    lax.fori_loop(1, heads_n, send_mlp, 0)

    even = lax.broadcasted_iota(jnp.int32, (own_slots, HEAD_DIM), 1) % 2 == 0
    even8 = even[:8]
    for j, gain_ref in enumerate((q_gain, k_gain)):
        gain = jnp.broadcast_to(gain_ref[...], (8, HEAD_DIM))
        swapped = swap_pairs(gain, even8)[0:1]
        table_c[j] = cosine[...] * gain_ref[...]
        table_s[j] = sine[...] * swapped

    def prepare(group):
        for block in range(3):
            where = pl.ds(pl.multiple_of(group * own_rows + block * own_slots, 8), own_slots)
            for j, target in enumerate((queries, keys)):
                raw = got_attn[group, block, j].astype(F32)
                for n in range(local_heads):
                    x = raw[:, n * HEAD_DIM : (n + 1) * HEAD_DIM]
                    r = lax.rsqrt(jnp.mean(x * x, axis=-1, keepdims=True) + 1e-06)
                    y = r * (x * table_c[j, where] + swap_pairs(x, even) * table_s[j, where])
                    target[n, where] = y
            raw = got_attn[group, block, 2].astype(F32)
            for n in range(local_heads):
                values[n, where] = raw[:, n * HEAD_DIM : (n + 1) * HEAD_DIM]

    def receive_attn(i, _):
        source = (head + heads_n - i) % heads_n
        attn_copy(i, head, source).wait_recv()
        prepare(source)
        return 0

    def activate(group):
        for block in range(3):
            where = pl.ds(pl.multiple_of(group * own_rows + block * own_slots, 8), own_slots)
            x = got_mlp[group, block].astype(F32)
            inner = math.sqrt(2.0 / math.pi) * (x + 0.044715 * (x * x * x))
            mlp_act[where] = 0.5 * x * (1.0 + jnp.tanh(inner))

    def receive_mlp(i, _):
        source = (head + heads_n - i) % heads_n
        mlp_copy(i, head, source).wait_recv()
        activate(source)
        return 0

    live = slot_number[...] < text_len[0]
    factor = math.log2(math.e) / math.sqrt(HEAD_DIM)
    band = rows // 3

    def attend(n):
        k = keys[n].astype(BF16)
        v = values[n].astype(BF16)
        for part in range(3):
            q = queries[n, pl.ds(part * band, band)].astype(BF16)
            scores = lax.dot_general(q, k, (((1,), (1,)), ((), ())), preferred_element_type=F32)
            scores = jnp.where(live, scores, -1e30)
            top = jnp.max(scores, axis=-1, keepdims=True)
            weight = jnp.exp2((scores - top) * factor)
            total = jnp.sum(weight, axis=-1, keepdims=True)
            mixed = jnp.dot(weight.astype(BF16), v, preferred_element_type=F32)
            act[pl.ds(part * band, band), n * HEAD_DIM : (n + 1) * HEAD_DIM] = (mixed / total).astype(BF16)

    locals_[0].wait()
    prepare(head)
    side_copy(cross, across, across).wait_recv()
    begin(1)
    lax.fori_loop(1, heads_n // 2, receive_attn, 0)
    advance(0, 1)
    advance(1, 1)
    lax.fori_loop(heads_n // 2, heads_n, receive_attn, 0)
    advance(0, 2)
    advance(1, 2)
    for n in range(local_heads):
        attend(n)
        if n == 1:
            advance(0, 3)
            advance(1, 3)
    locals_[1].wait()
    activate(head)
    lax.fori_loop(1, heads_n, receive_mlp, 0)
    act[:, width:] = mlp_act[...].astype(BF16)
    advance(0, 4)
    advance(1, 4)
    for stream_ in (0, 1):
        for offset in range(z_n):
            slot = tile_at(half_of(stream_), (depth + offset) % z_n, 1 - core)
            side_copy(stream_ * z_n + offset, slot, sibling).wait_recv()

    def part_copy(chunk, i, peer, source):
        return pltpu.make_async_remote_copy(
            src_ref=outgoing.at[chunk, peer],
            dst_ref=incoming.at[chunk, source],
            send_sem=part_send.at[chunk, i],
            recv_sem=part_recv.at[chunk, i],
            device_id={"head": peer},
            device_id_type=MESH,
        )

    def project(chunk, _):
        block = weights[pl.ds(chunk * per_chunk, per_chunk)].reshape(columns, width + units)
        product[...] = lax.dot_general(
            act[...], block, (((1,), (1,)), ((), ())), preferred_element_type=F32
        )

        def send_part(i, _):
            peer = (head + i) % heads_n
            part = product[pl.ds(pl.multiple_of(peer * own_rows, 8), own_rows)]
            outgoing[chunk, peer] = part.astype(BF16)
            part_copy(chunk, i, peer, head).start()
            return 0

        lax.fori_loop(1, heads_n, send_part, 0)
        mine[chunk] = product[pl.ds(pl.multiple_of(head * own_rows, 8), own_rows)]
        return 0

    lax.fori_loop(0, chunks, project, 0)

    locals_[4].wait()
    locals_[5].wait()

    def collect(chunk, _):
        at = pl.ds(pl.multiple_of(chunk * columns, 128), columns)

        def wait_part(i, _):
            part_copy(chunk, i, head, (head + heads_n - i) % heads_n).wait_recv()
            return 0

        lax.fori_loop(1, heads_n, wait_part, 0)
        total = mine[chunk]
        for i in range(1, heads_n):
            total = total + incoming[chunk, (head + i) % heads_n].astype(F32)
        for block in range(3):
            part = slice(block * own_slots, (block + 1) * own_slots)
            new = stream[block, :, at].astype(F32) + gate[:, at] * (total[part] + bias_out[:, at])
            updated[block, :, at] = new
            hidden_out[block, :, at] = new.astype(BF16)
        return 0

    lax.fori_loop(0, chunks, collect, 0)

    for block in (1, 2):
        image = updated[block]
        center = image - jnp.mean(image, axis=-1, keepdims=True)
        variance = jnp.mean(center * center, axis=-1, keepdims=True)
        normed = center * lax.rsqrt(variance + 1e-06)
        modulated = ((1.0 + scale[...]) * normed + shift[...]).astype(BF16)
        velocity = lax.dot_general(
            modulated, final_w[...], (((1,), (1,)), ((), ())), preferred_element_type=F32
        )
        latent_out[block - 1] = latent[block - 1] + step_size[0] * (velocity + b_final[...])

    def drain(i, _):
        attn_copy(i, (head + i) % heads_n, head).wait_send()
        mlp_copy(i, (head + i) % heads_n, head).wait_send()
        return 0

    lax.fori_loop(1, heads_n, drain, 0)

    def drain_parts(chunk, _):
        def one(i, _):
            part_copy(chunk, i, (head + i) % heads_n, head).wait_send()
            return 0

        lax.fori_loop(1, heads_n, one, 0)
        return 0

    lax.fori_loop(0, chunks, drain_parts, 0)
    side_copy(cross, tile, across).wait_send()
    for stream_ in (0, 1):
        for offset in range(z_n):
            slot = tile_at(half_of(stream_), (depth + offset) % z_n, core)
            side_copy(stream_ * z_n + offset, slot, sibling).wait_send()
        for direction in (0, 1):
            for step in range(1, reach[direction] + 1):
                offset = z_n - step + 1 if direction == 0 else step - 1
                slot = tile_at(half_of(stream_), (depth + offset) % z_n, core)
                ring_copy(stream_, direction, step, slot).wait_send()


def solution(mesh):
    heads_n = mesh.shape["head"]
    tiles_n = mesh.shape["tile"]
    z_n = tiles_n // 4
    chunks = 8
    cosine, sine, slot_number = rope_constants(heads_n)

    def per_device(
        attn_proj,
        mlp_proj,
        stream,
        text_len,
        q_gain,
        k_gain,
        w_out_attn,
        w_out_mlp,
        bias_out,
        gate_mod,
        final_shift,
        final_scale,
        w_final,
        b_final,
        latent,
        step_size,
    ):
        own_slots = attn_proj.shape[2]
        own_rows = 3 * own_slots
        rows = heads_n * own_rows
        features = attn_proj.shape[4]
        width, shard = w_out_attn.shape
        units = w_out_mlp.shape[0]
        local_heads = width // HEAD_DIM
        columns = features // chunks
        channels = w_final.shape[1]
        cfg = (heads_n, z_n, chunks, own_rows, own_slots)
        any_ = pl.BlockSpec(memory_space=pl.ANY)
        vmem = pl.BlockSpec(memory_space=pltpu.VMEM)
        smem = pl.BlockSpec(memory_space=pltpu.SMEM)
        dma = pltpu.SemaphoreType.DMA
        hidden, latent_next = pl.pallas_call(
            functools.partial(layer_kernel, cfg),
            out_shape=(
                jax.ShapeDtypeStruct((3, own_slots, features), BF16),
                jax.ShapeDtypeStruct((2, own_slots, channels), F32),
            ),
            in_specs=[smem, smem] + [any_] * 6 + [vmem] * 11,
            out_specs=(vmem, vmem),
            scratch_shapes=[
                pltpu.VMEM((heads_n, 3, 3, own_slots, width), BF16),
                pltpu.VMEM((heads_n, 3, own_slots, units), BF16),
                pltpu.VMEM((tiles_n, shard, width + units), BF16),
                pltpu.VMEM((local_heads, rows, HEAD_DIM), F32),
                pltpu.VMEM((local_heads, rows, HEAD_DIM), F32),
                pltpu.VMEM((local_heads, rows, HEAD_DIM), F32),
                pltpu.VMEM((rows, units), F32),
                pltpu.VMEM((rows, width + units), BF16),
                pltpu.VMEM((rows, columns), F32),
                pltpu.VMEM((chunks, heads_n, own_rows, columns), BF16),
                pltpu.VMEM((chunks, heads_n, own_rows, columns), BF16),
                pltpu.VMEM((chunks, own_rows, columns), F32),
                pltpu.VMEM((3, own_slots, features), F32),
                pltpu.VMEM((3, own_slots, features), BF16),
                pltpu.VMEM((channels, features), BF16),
                pltpu.VMEM((2, rows, HEAD_DIM), F32),
                pltpu.VMEM((2, rows, HEAD_DIM), F32),
                dma((6,)),
                dma((heads_n,)),
                dma((heads_n,)),
                dma((heads_n,)),
                dma((heads_n,)),
                dma((2, 2, z_n)),
                dma((2, 2, z_n)),
                dma((2 * z_n + 1,)),
                dma((2 * z_n + 1,)),
                dma((chunks, heads_n)),
                dma((chunks, heads_n)),
            ],
            compiler_params=pltpu.CompilerParams(
                collective_id=0, has_side_effects=True, vmem_limit_bytes=56 * 1024 * 1024
            ),
        )(
            text_len,
            step_size,
            jnp.transpose(attn_proj[0], (0, 2, 1, 3)),
            mlp_proj[0],
            stream[0],
            w_out_attn.T,
            w_out_mlp.T,
            w_final.T,
            jnp.asarray(cosine.reshape(rows, HEAD_DIM)),
            jnp.asarray(sine.reshape(rows, HEAD_DIM)),
            jnp.asarray(slot_number),
            q_gain[None],
            k_gain[None],
            bias_out[None],
            gate_mod,
            final_shift,
            final_scale,
            b_final[None],
            latent[0],
        )
        return hidden[None], latent_next[None]

    placed = (
        P("tile", None, "head", None, None),
        P("tile", None, "head", None),
        P("tile", None, "head", None),
        P("tile"),
        P(),
        P(),
        P("head", "tile"),
        P("head", "tile"),
        P(),
        P("tile", None),
        P("tile", None),
        P("tile", None),
        P(),
        P(),
        P("tile", None, "head", None),
        P("tile"),
    )
    return jax.shard_map(
        per_device,
        mesh=mesh,
        in_specs=placed,
        out_specs=(P("tile", None, "head", None), P("tile", None, "head", None)),
        check_vma=False,
    )
```

profile of v0, /device:TPU:1, one launch (start us, length us, event | category | flops | bytes accessed | tf_op | source)
XLA Modules:
  0.0 118.9 jit_solution(12474661164591180934)
XLA Ops:
  1.9 113.8 %shard_map.194 = (bf16[3,24,3072]{2,1,0:T(8,128)(2,1)}, f32[2,24,64]{2,1,0:T(8,128)}) custom-call(s32[1]{0:T(128)S(6)} %copy.23.text_len, f32[1]{0:T(128)S(6)} %copy.24.step_size, bf16[3,3,24,3072]{3,2,1,0:T(8,128)(2,1)} %bitcast.15, bf16[3,24,6144]{2,1,0:T(8,128)(2,1)} %bitcast.16, bf16[3,24,3072]{2,1,0:T(8,128)(2,1)} %bitcast.17, ...), custom_call_target="tpu_custom_call" | custom-call | tf_op jit(solution)/shard_map/pallas_call | solution.py:442
  115.7 1.8 %copy.25 = bf16[1,3,24,3072]{3,2,1,0:T(8,128)(2,1)} copy(bf16[1,3,24,3072]{3,2,1,0:T(8,128)(2,1)} %bitcast.18) | data formatting | bytes 884736
  117.5 1.3 %copy.26 = f32[1,2,24,64]{3,2,1,0:T(8,128)} copy(f32[1,2,24,64]{3,2,1,0:T(8,128)} %bitcast.23) | data formatting | bytes 24576
where the time goes:
time: 119 us
  Pallas kernels  114 us (96%)
  local copies, waits for them, and re-layouts  3.15 us (3%)
  between operations  1.94 us (2%)
    pallas_call x1, Pallas kernels, per_device(): pl.pallas_call(functools.partial(layer_kernel, cfg), out_shape=(jax.Shape...  114 us
    unnamed x2, local copies, waits for them, and re-layouts  3.15 us

commit v1 on v0

--- a/solution.py
+++ b/solution.py
@@ -74,8 +74,14 @@
     mlp_act,
     act,
     product,
-    outgoing,
-    incoming,
+    y_out,
+    y_in,
+    y_pass,
+    y_got,
+    x_out,
+    x_in,
+    x_pass,
+    x_got,
     mine,
     updated,
     stream,
@@ -91,20 +97,29 @@
     ring_recv,
     side_send,
     side_recv,
-    part_send,
-    part_recv,
+    y_send,
+    y_recv,
+    y_pass_send,
+    y_pass_recv,
+    x_send,
+    x_recv,
+    x_pass_send,
+    x_pass_recv,
 ):
-    heads_n, z_n, chunks, own_rows, own_slots = cfg
+    heads_n, z_n, pairs, own_rows, own_slots = cfg
+    y_n = heads_n // 2
     tile = lax.axis_index("tile")
     head = lax.axis_index("head")
     core = tile % 2
     depth = (tile // 2) % z_n
     half = tile // (2 * z_n)
+    row_y = head // 2
+    side_x = head % 2
     width = got_attn.shape[4]
     units = got_mlp.shape[3]
     local_heads = width // HEAD_DIM
     shard = weights.shape[1]
-    per_chunk = weights.shape[0] // chunks
+    per_chunk = weights.shape[0] // (2 * pairs)
     columns = shard * per_chunk
     rows = heads_n * own_rows
 
@@ -115,6 +130,15 @@
     down = tile_at(half, (depth + z_n - 1) % z_n, core)
     across = tile_at(1 - half, depth, core)
     sibling = tile_at(half, depth, 1 - core)
+
+    def head_at(dy, dx):
+        return ((row_y + dy + y_n) % y_n) * 2 + (side_x + dx) % 2
+
+    def peer_of(i):
+        return head_at(i // 2, i % 2)
+
+    def source_of(i):
+        return head_at(-(i // 2), i % 2)
 
     def local_copies():
         at = pl.ds(pl.multiple_of(head * width, width), width)
@@ -136,7 +160,7 @@
         pl.semaphore_signal(barrier, inc=1, device_id={"tile": neighbour}, device_id_type=MESH)
 
     def greet(i, _):
-        pl.semaphore_signal(barrier, inc=1, device_id={"head": (head + i) % heads_n}, device_id_type=MESH)
+        pl.semaphore_signal(barrier, inc=1, device_id={"head": peer_of(i)}, device_id_type=MESH)
         return 0
 
     lax.fori_loop(1, heads_n, greet, 0)
@@ -163,14 +187,12 @@
         )
 
     def send_attn(i, _):
-        attn_copy(i, (head + i) % heads_n, head).start()
+        attn_copy(i, peer_of(i), head).start()
         return 0
 
     def send_mlp(i, _):
-        mlp_copy(i, (head + i) % heads_n, head).start()
-        return 0
-
-    lax.fori_loop(1, heads_n, send_attn, 0)
+        mlp_copy(i, peer_of(i), head).start()
+        return 0
 
     def ring_copy(stream_, direction, step, slot):
         return pltpu.make_async_remote_copy(
@@ -192,7 +214,8 @@
             device_id_type=MESH,
         )
 
-    reach = (z_n // 2, z_n - 1 - z_n // 2)
+    far, near = z_n // 2, z_n - 1 - z_n // 2
+    reach = ((far, near), (near, far))
 
     def half_of(stream_):
         return half if stream_ == 0 else 1 - half
@@ -210,10 +233,10 @@
 
     def advance(stream_, step):
         for direction in (0, 1):
-            if step <= reach[direction]:
+            if step <= reach[stream_][direction]:
                 slot, number = arrival(stream_, direction, step)
                 ring_copy(stream_, direction, step, slot).wait_recv()
-                if step < reach[direction]:
+                if step < reach[stream_][direction]:
                     ring_copy(stream_, direction, step + 1, slot).start()
                 side_copy(number, slot, sibling).start()
 
@@ -223,6 +246,7 @@
     locals_[3].wait()
     side_copy(cross, tile, across).start()
     begin(0)
+    lax.fori_loop(1, heads_n, send_attn, 0)
     lax.fori_loop(1, heads_n, send_mlp, 0)
 
     even = lax.broadcasted_iota(jnp.int32, (own_slots, HEAD_DIM), 1) % 2 == 0
@@ -248,7 +272,7 @@
                 values[n, where] = raw[:, n * HEAD_DIM : (n + 1) * HEAD_DIM]
 
     def receive_attn(i, _):
-        source = (head + heads_n - i) % heads_n
+        source = source_of(i)
         attn_copy(i, head, source).wait_recv()
         prepare(source)
         return 0
@@ -261,7 +285,7 @@
             mlp_act[where] = 0.5 * x * (1.0 + jnp.tanh(inner))
 
     def receive_mlp(i, _):
-        source = (head + heads_n - i) % heads_n
+        source = source_of(i)
         mlp_copy(i, head, source).wait_recv()
         activate(source)
         return 0
@@ -295,71 +319,155 @@
     advance(1, 2)
     for n in range(local_heads):
         attend(n)
-        if n == 1:
-            advance(0, 3)
-            advance(1, 3)
     locals_[1].wait()
     activate(head)
     lax.fori_loop(1, heads_n, receive_mlp, 0)
     act[:, width:] = mlp_act[...].astype(BF16)
-    advance(0, 4)
-    advance(1, 4)
-    for stream_ in (0, 1):
-        for offset in range(z_n):
-            slot = tile_at(half_of(stream_), (depth + offset) % z_n, 1 - core)
-            side_copy(stream_ * z_n + offset, slot, sibling).wait_recv()
-
-    def part_copy(chunk, i, peer, source):
-        return pltpu.make_async_remote_copy(
-            src_ref=outgoing.at[chunk, peer],
-            dst_ref=incoming.at[chunk, source],
-            send_sem=part_send.at[chunk, i],
-            recv_sem=part_recv.at[chunk, i],
-            device_id={"head": peer},
-            device_id_type=MESH,
-        )
-
-    def project(chunk, _):
-        block = weights[pl.ds(chunk * per_chunk, per_chunk)].reshape(columns, width + units)
-        product[...] = lax.dot_general(
-            act[...], block, (((1,), (1,)), ((), ())), preferred_element_type=F32
-        )
-
-        def send_part(i, _):
-            peer = (head + i) % heads_n
-            part = product[pl.ds(pl.multiple_of(peer * own_rows, 8), own_rows)]
-            outgoing[chunk, peer] = part.astype(BF16)
-            part_copy(chunk, i, peer, head).start()
-            return 0
-
-        lax.fori_loop(1, heads_n, send_part, 0)
-        mine[chunk] = product[pl.ds(pl.multiple_of(head * own_rows, 8), own_rows)]
-        return 0
-
-    lax.fori_loop(0, chunks, project, 0)
-
     locals_[4].wait()
     locals_[5].wait()
 
-    def collect(chunk, _):
-        at = pl.ds(pl.multiple_of(chunk * columns, 128), columns)
-
-        def wait_part(i, _):
-            part_copy(chunk, i, head, (head + heads_n - i) % heads_n).wait_recv()
-            return 0
-
-        lax.fori_loop(1, heads_n, wait_part, 0)
-        total = mine[chunk]
-        for i in range(1, heads_n):
-            total = total + incoming[chunk, (head + i) % heads_n].astype(F32)
+    def wait_sibling(offsets):
+        for stream_ in (0, 1):
+            for offset in offsets:
+                slot = tile_at(half_of(stream_), (depth + offset) % z_n, 1 - core)
+                side_copy(stream_ * z_n + offset, slot, sibling).wait_recv()
+
+    def y_copy(p, dy, peer_y):
+        return pltpu.make_async_remote_copy(
+            src_ref=y_out.at[p, peer_y],
+            dst_ref=y_in.at[p, dy],
+            send_sem=y_send.at[p, dy],
+            recv_sem=y_recv.at[p, dy],
+            device_id={"head": peer_y * 2 + side_x},
+            device_id_type=MESH,
+        )
+
+    def y_pass_copy(p):
+        return pltpu.make_async_remote_copy(
+            src_ref=y_pass.at[p],
+            dst_ref=y_got.at[p],
+            send_sem=y_pass_send.at[p],
+            recv_sem=y_pass_recv.at[p],
+            device_id={"head": head_at(0, 1)},
+            device_id_type=MESH,
+        )
+
+    def x_copy(p):
+        return pltpu.make_async_remote_copy(
+            src_ref=x_out.at[p],
+            dst_ref=x_in.at[p],
+            send_sem=x_send.at[p],
+            recv_sem=x_recv.at[p],
+            device_id={"head": head_at(0, 1)},
+            device_id_type=MESH,
+        )
+
+    def x_pass_copy(p, dy):
+        return pltpu.make_async_remote_copy(
+            src_ref=x_pass.at[p, dy],
+            dst_ref=x_got.at[p, dy],
+            send_sem=x_pass_send.at[p, dy],
+            recv_sem=x_pass_recv.at[p, dy],
+            device_id={"head": head_at(dy, 0)},
+            device_id_type=MESH,
+        )
+
+    def group_rows(kind, p, group):
+        return product[kind, p, pl.ds(pl.multiple_of(group * own_rows, 8), own_rows)]
+
+    def chunk_of(kind, p):
+        order = p + (p // 2) * (1 - 2 * (p % 2))
+        return kind * pairs + (depth // 2 + order) % pairs
+
+    def pass_on(p):
+        for dy in range(1, y_n):
+            y_copy(p, dy, row_y).wait_recv()
+        for dx in (0, 1):
+            side = (side_x + dx) % 2
+            total = group_rows(0, p, row_y * 2 + side)
+            for dy in range(1, y_n):
+                total = total + y_in[p, dy, side].astype(F32)
+            if dx == 0:
+                mine[0, p] = total
+            else:
+                y_pass[p] = total.astype(BF16)
+        y_pass_copy(p).start()
+        x_copy(p).wait_recv()
+        for dy in range(1, y_n):
+            peer_y = (row_y + dy) % y_n
+            total = group_rows(1, p, peer_y * 2 + side_x) + x_in[p, peer_y].astype(F32)
+            x_pass[p, dy] = total.astype(BF16)
+            x_pass_copy(p, dy).start()
+        mine[1, p] = group_rows(1, p, head) + x_in[p, row_y].astype(F32)
+
+    wait_sibling([0] + [o for o in (1, z_n - 1) if o != 0])
+
+    def project(k, _):
+        p, kind = k // 2, k % 2
+
+        @pl.when(k == 2)
+        def _():
+            for step in range(3, far):
+                advance(0, step)
+                advance(1, step)
+            wait_sibling([o for o in range(2, z_n - 1) if o != far])
+
+        @pl.when(k == 2 * pairs - 2)
+        def _():
+            pass_on(0)
+            advance(0, far)
+            advance(1, far)
+            wait_sibling([far])
+
+        block = weights[pl.ds(chunk_of(kind, p) * per_chunk, per_chunk)].reshape(columns, width + units)
+        product[kind, p] = lax.dot_general(
+            act[...], block, (((1,), (1,)), ((), ())), preferred_element_type=F32
+        )
+
+        @pl.when(kind == 0)
+        def _():
+            for dy in range(1, y_n):
+                peer_y = (row_y + dy) % y_n
+                for side in (0, 1):
+                    y_out[p, peer_y, side] = group_rows(0, p, peer_y * 2 + side).astype(BF16)
+                y_copy(p, dy, peer_y).start()
+
+        @pl.when(kind == 1)
+        def _():
+            for peer_y in range(y_n):
+                x_out[p, peer_y] = group_rows(1, p, peer_y * 2 + 1 - side_x).astype(BF16)
+            x_copy(p).start()
+
+        return 0
+
+    lax.fori_loop(0, 2 * pairs, project, 0)
+
+    def store(kind, p, total):
+        at = pl.ds(pl.multiple_of(chunk_of(kind, p) * columns, 128), columns)
         for block in range(3):
             part = slice(block * own_slots, (block + 1) * own_slots)
             new = stream[block, :, at].astype(F32) + gate[:, at] * (total[part] + bias_out[:, at])
             updated[block, :, at] = new
             hidden_out[block, :, at] = new.astype(BF16)
-        return 0
-
-    lax.fori_loop(0, chunks, collect, 0)
+
+    def collect(p):
+        y_pass_copy(p).wait_recv()
+        store(0, p, mine[0, p] + y_got[p].astype(F32))
+        total = mine[1, p]
+        for dy in range(1, y_n):
+            x_pass_copy(p, dy).wait_recv()
+            total = total + x_got[p, dy].astype(F32)
+        store(1, p, total)
+
+    def finish(p, _):
+        @pl.when(p < pairs)
+        def _():
+            pass_on(p)
+
+        collect(p - 1)
+        return 0
+
+    lax.fori_loop(1, pairs + 1, finish, 0)
 
     for block in (1, 2):
         image = updated[block]
@@ -373,28 +481,28 @@
         latent_out[block - 1] = latent[block - 1] + step_size[0] * (velocity + b_final[...])
 
     def drain(i, _):
-        attn_copy(i, (head + i) % heads_n, head).wait_send()
-        mlp_copy(i, (head + i) % heads_n, head).wait_send()
+        attn_copy(i, peer_of(i), head).wait_send()
+        mlp_copy(i, peer_of(i), head).wait_send()
         return 0
 
     lax.fori_loop(1, heads_n, drain, 0)
 
-    def drain_parts(chunk, _):
-        def one(i, _):
-            part_copy(chunk, i, (head + i) % heads_n, head).wait_send()
-            return 0
-
-        lax.fori_loop(1, heads_n, one, 0)
-        return 0
-
-    lax.fori_loop(0, chunks, drain_parts, 0)
+    def drain_parts(p, _):
+        for dy in range(1, y_n):
+            y_copy(p, dy, (row_y + dy) % y_n).wait_send()
+            x_pass_copy(p, dy).wait_send()
+        y_pass_copy(p).wait_send()
+        x_copy(p).wait_send()
+        return 0
+
+    lax.fori_loop(0, pairs, drain_parts, 0)
     side_copy(cross, tile, across).wait_send()
     for stream_ in (0, 1):
         for offset in range(z_n):
             slot = tile_at(half_of(stream_), (depth + offset) % z_n, core)
             side_copy(stream_ * z_n + offset, slot, sibling).wait_send()
         for direction in (0, 1):
-            for step in range(1, reach[direction] + 1):
+            for step in range(1, reach[stream_][direction] + 1):
                 offset = z_n - step + 1 if direction == 0 else step - 1
                 slot = tile_at(half_of(stream_), (depth + offset) % z_n, core)
                 ring_copy(stream_, direction, step, slot).wait_send()
@@ -404,7 +512,7 @@
     heads_n = mesh.shape["head"]
     tiles_n = mesh.shape["tile"]
     z_n = tiles_n // 4
-    chunks = 8
+    pairs = 4
     cosine, sine, slot_number = rope_constants(heads_n)
 
     def per_device(
@@ -432,9 +540,10 @@
         width, shard = w_out_attn.shape
         units = w_out_mlp.shape[0]
         local_heads = width // HEAD_DIM
-        columns = features // chunks
+        columns = features // (2 * pairs)
+        y_n = heads_n // 2
         channels = w_final.shape[1]
-        cfg = (heads_n, z_n, chunks, own_rows, own_slots)
+        cfg = (heads_n, z_n, pairs, own_rows, own_slots)
         any_ = pl.BlockSpec(memory_space=pl.ANY)
         vmem = pl.BlockSpec(memory_space=pltpu.VMEM)
         smem = pl.BlockSpec(memory_space=pltpu.SMEM)
@@ -456,10 +565,16 @@
                 pltpu.VMEM((local_heads, rows, HEAD_DIM), F32),
                 pltpu.VMEM((rows, units), F32),
                 pltpu.VMEM((rows, width + units), BF16),
-                pltpu.VMEM((rows, columns), F32),
-                pltpu.VMEM((chunks, heads_n, own_rows, columns), BF16),
-                pltpu.VMEM((chunks, heads_n, own_rows, columns), BF16),
-                pltpu.VMEM((chunks, own_rows, columns), F32),
+                pltpu.VMEM((2, pairs, rows, columns), F32),
+                pltpu.VMEM((pairs, y_n, 2, own_rows, columns), BF16),
+                pltpu.VMEM((pairs, y_n, 2, own_rows, columns), BF16),
+                pltpu.VMEM((pairs, own_rows, columns), BF16),
+                pltpu.VMEM((pairs, own_rows, columns), BF16),
+                pltpu.VMEM((pairs, y_n, own_rows, columns), BF16),
+                pltpu.VMEM((pairs, y_n, own_rows, columns), BF16),
+                pltpu.VMEM((pairs, y_n, own_rows, columns), BF16),
+                pltpu.VMEM((pairs, y_n, own_rows, columns), BF16),
+                pltpu.VMEM((2, pairs, own_rows, columns), F32),
                 pltpu.VMEM((3, own_slots, features), F32),
                 pltpu.VMEM((3, own_slots, features), BF16),
                 pltpu.VMEM((channels, features), BF16),
@@ -474,8 +589,14 @@
                 dma((2, 2, z_n)),
                 dma((2 * z_n + 1,)),
                 dma((2 * z_n + 1,)),
-                dma((chunks, heads_n)),
-                dma((chunks, heads_n)),
+                dma((pairs, y_n)),
+                dma((pairs, y_n)),
+                dma((pairs,)),
+                dma((pairs,)),
+                dma((pairs,)),
+                dma((pairs,)),
+                dma((pairs, y_n)),
+                dma((pairs, y_n)),
             ],
             compiler_params=pltpu.CompilerParams(
                 collective_id=0, has_side_effects=True, vmem_limit_bytes=56 * 1024 * 1024

time: 119 us -> 85 us (0.71)
  Pallas kernels: 114 us -> 79.7 us
    pallas_call x1, Pallas kernels: 114 us -> 79.7 us  [per_device(): pl.pallas_call(functools.partial(layer_kernel, cfg), out_shape=(jax.Shape...]
where the time goes in v1:
time: 85 us; the launch traced here: 84.7 us
  Pallas kernels  79.7 us (94%)
  local copies, waits for them, and re-layouts  3.15 us (4%)
  between operations  1.94 us (2%)
    pallas_call x1, Pallas kernels, per_device(): pl.pallas_call(functools.partial(layer_kernel, cfg), out_shape=(jax.Shape...  79.7 us
    unnamed x2, local copies, waits for them, and re-layouts  3.15 us

profile of v1, /device:TPU:1, one launch (start us, length us, event | category | flops | bytes accessed | tf_op | source)
XLA Modules:
  0.0 84.7 jit_solution(11481717578811574861)
XLA Ops:
  1.9 79.7 %shard_map.194 = (bf16[3,24,3072]{2,1,0:T(8,128)(2,1)}, f32[2,24,64]{2,1,0:T(8,128)}) custom-call(s32[1]{0:T(128)S(6)} %copy.23.text_len, f32[1]{0:T(128)S(6)} %copy.24.step_size, bf16[3,3,24,3072]{3,2,1,0:T(8,128)(2,1)} %bitcast.15, bf16[3,24,6144]{2,1,0:T(8,128)(2,1)} %bitcast.16, bf16[3,24,3072]{2,1,0:T(8,128)(2,1)} %bitcast.17, ...), custom_call_target="tpu_custom_call" | custom-call | tf_op jit(solution)/shard_map/pallas_call | solution.py:551
  81.6 1.8 %copy.25 = bf16[1,3,24,3072]{3,2,1,0:T(8,128)(2,1)} copy(bf16[1,3,24,3072]{3,2,1,0:T(8,128)(2,1)} %bitcast.18) | data formatting | bytes 884736
  83.4 1.3 %copy.26 = f32[1,2,24,64]{3,2,1,0:T(8,128)} copy(f32[1,2,24,64]{3,2,1,0:T(8,128)} %bitcast.23) | data formatting | bytes 24576

commit v2 on v1

--- a/solution.py
+++ b/solution.py
@@ -119,13 +119,16 @@
     units = got_mlp.shape[3]
     local_heads = width // HEAD_DIM
     shard = weights.shape[1]
-    per_chunk = weights.shape[0] // (2 * pairs)
-    columns = shard * per_chunk
+    columns = shard * 4
     rows = heads_n * own_rows
 
     def tile_at(half_, depth_, core_):
         return half_ * (2 * z_n) + depth_ * 2 + core_
 
+    def shard_at(half_, depth_, core_):
+        return depth_ * 4 + half_ * 2 + core_
+
+    own_shard = shard_at(half, depth, core)
     up = tile_at(half, (depth + 1) % z_n, core)
     down = tile_at(half, (depth + z_n - 1) % z_n, core)
     across = tile_at(1 - half, depth, core)
@@ -146,8 +149,8 @@
         return [
             pltpu.make_async_copy(attn_in.at[:, :, :, at], got_attn.at[head], local_sem.at[0]),
             pltpu.make_async_copy(mlp_in.at[:, :, mt], got_mlp.at[head], local_sem.at[1]),
-            pltpu.make_async_copy(weight_attn, weights.at[tile, :, pl.ds(0, width)], local_sem.at[2]),
-            pltpu.make_async_copy(weight_mlp, weights.at[tile, :, pl.ds(width, units)], local_sem.at[3]),
+            pltpu.make_async_copy(weight_attn, weights.at[own_shard, :, pl.ds(0, width)], local_sem.at[2]),
+            pltpu.make_async_copy(weight_mlp, weights.at[own_shard, :, pl.ds(width, units)], local_sem.at[3]),
             pltpu.make_async_copy(stream_in, stream, local_sem.at[4]),
             pltpu.make_async_copy(w_final, final_w, local_sem.at[5]),
         ]
@@ -222,11 +225,11 @@
 
     def arrival(stream_, direction, step):
         offset = z_n - step if direction == 0 else step
-        slot = tile_at(half_of(stream_), (depth + offset) % z_n, core)
+        slot = shard_at(half_of(stream_), (depth + offset) % z_n, core)
         return slot, stream_ * z_n + (offset if offset < z_n else 0)
 
     def begin(stream_):
-        slot = tile_at(half_of(stream_), depth, core)
+        slot = shard_at(half_of(stream_), depth, core)
         ring_copy(stream_, 0, 1, slot).start()
         ring_copy(stream_, 1, 1, slot).start()
         side_copy(stream_ * z_n, slot, sibling).start()
@@ -244,7 +247,7 @@
     locals_ = local_copies()
     locals_[2].wait()
     locals_[3].wait()
-    side_copy(cross, tile, across).start()
+    side_copy(cross, own_shard, across).start()
     begin(0)
     lax.fori_loop(1, heads_n, send_attn, 0)
     lax.fori_loop(1, heads_n, send_mlp, 0)
@@ -309,11 +312,11 @@
 
     locals_[0].wait()
     prepare(head)
-    side_copy(cross, across, across).wait_recv()
+    side_copy(cross, shard_at(1 - half, depth, core), across).wait_recv()
     begin(1)
-    lax.fori_loop(1, heads_n // 2, receive_attn, 0)
     advance(0, 1)
     advance(1, 1)
+    lax.fori_loop(1, heads_n // 2, receive_attn, 0)
     lax.fori_loop(heads_n // 2, heads_n, receive_attn, 0)
     advance(0, 2)
     advance(1, 2)
@@ -329,7 +332,7 @@
     def wait_sibling(offsets):
         for stream_ in (0, 1):
             for offset in offsets:
-                slot = tile_at(half_of(stream_), (depth + offset) % z_n, 1 - core)
+                slot = shard_at(half_of(stream_), (depth + offset) % z_n, 1 - core)
                 side_copy(stream_ * z_n + offset, slot, sibling).wait_recv()
 
     def y_copy(p, dy, peer_y):
@@ -375,9 +378,8 @@
     def group_rows(kind, p, group):
         return product[kind, p, pl.ds(pl.multiple_of(group * own_rows, 8), own_rows)]
 
-    def chunk_of(kind, p):
-        order = p + (p // 2) * (1 - 2 * (p % 2))
-        return kind * pairs + (depth // 2 + order) % pairs
+    def offset_of(kind, p):
+        return p + 1 if kind == 1 else (z_n - p) % z_n
 
     def pass_on(p):
         for dy in range(1, y_n):
@@ -400,26 +402,32 @@
             x_pass_copy(p, dy).start()
         mine[1, p] = group_rows(1, p, head) + x_in[p, row_y].astype(F32)
 
-    wait_sibling([0] + [o for o in (1, z_n - 1) if o != 0])
+    wait_sibling([offset_of(kind, 0) for kind in (0, 1)])
 
     def project(k, _):
         p, kind = k // 2, k % 2
 
         @pl.when(k == 2)
         def _():
+            wait_sibling([offset_of(kind, 1) for kind in (0, 1)])
             for step in range(3, far):
                 advance(0, step)
                 advance(1, step)
-            wait_sibling([o for o in range(2, z_n - 1) if o != far])
+
+        @pl.when(k == 4)
+        def _():
+            wait_sibling([offset_of(kind, p) for p in range(2, pairs - 1) for kind in (0, 1)])
 
         @pl.when(k == 2 * pairs - 2)
         def _():
             pass_on(0)
             advance(0, far)
             advance(1, far)
-            wait_sibling([far])
-
-        block = weights[pl.ds(chunk_of(kind, p) * per_chunk, per_chunk)].reshape(columns, width + units)
+            wait_sibling([offset_of(kind, pairs - 1) for kind in (0, 1)])
+
+        offset = kind * (p + 1) + (1 - kind) * ((z_n - p) % z_n)
+        nearest = (depth + offset) % z_n
+        block = weights[pl.ds(nearest * 4, 4)].reshape(columns, width + units)
         product[kind, p] = lax.dot_general(
             act[...], block, (((1,), (1,)), ((), ())), preferred_element_type=F32
         )
@@ -442,22 +450,14 @@
 
     lax.fori_loop(0, 2 * pairs, project, 0)
 
-    def store(kind, p, total):
-        at = pl.ds(pl.multiple_of(chunk_of(kind, p) * columns, 128), columns)
-        for block in range(3):
-            part = slice(block * own_slots, (block + 1) * own_slots)
-            new = stream[block, :, at].astype(F32) + gate[:, at] * (total[part] + bias_out[:, at])
-            updated[block, :, at] = new
-            hidden_out[block, :, at] = new.astype(BF16)
-
     def collect(p):
         y_pass_copy(p).wait_recv()
-        store(0, p, mine[0, p] + y_got[p].astype(F32))
+        mine[0, p] = mine[0, p] + y_got[p].astype(F32)
         total = mine[1, p]
         for dy in range(1, y_n):
             x_pass_copy(p, dy).wait_recv()
             total = total + x_got[p, dy].astype(F32)
-        store(1, p, total)
+        mine[1, p] = total
 
     def finish(p, _):
         @pl.when(p < pairs)
@@ -468,6 +468,26 @@
         return 0
 
     lax.fori_loop(1, pairs + 1, finish, 0)
+
+    def sum_at(z):
+        offset = (z + z_n - depth) % z_n
+        kind = (offset + z_n - 1) % z_n // pairs
+        p = (1 - kind) * (offset - 1) + kind * ((z_n - offset) % z_n)
+        return mine[1 - kind, p]
+
+    narrow = columns // 2
+    for pair in range(z_n // 2):
+        low, high = sum_at(2 * pair), sum_at(2 * pair + 1)
+        for side in (0, 1):
+            piece = slice(side * narrow, (side + 1) * narrow)
+            total = jnp.concatenate([low[:, piece], high[:, piece]], axis=-1)
+            start = side * narrow * z_n + pair * columns
+            at = slice(start, start + columns)
+            for block in range(3):
+                part = slice(block * own_slots, (block + 1) * own_slots)
+                new = stream[block, :, at].astype(F32) + gate[:, at] * (total[part] + bias_out[:, at])
+                updated[block, :, at] = new
+                hidden_out[block, :, at] = new.astype(BF16)
 
     for block in (1, 2):
         image = updated[block]
@@ -496,15 +516,15 @@
         return 0
 
     lax.fori_loop(0, pairs, drain_parts, 0)
-    side_copy(cross, tile, across).wait_send()
+    side_copy(cross, own_shard, across).wait_send()
     for stream_ in (0, 1):
         for offset in range(z_n):
-            slot = tile_at(half_of(stream_), (depth + offset) % z_n, core)
+            slot = shard_at(half_of(stream_), (depth + offset) % z_n, core)
             side_copy(stream_ * z_n + offset, slot, sibling).wait_send()
         for direction in (0, 1):
             for step in range(1, reach[stream_][direction] + 1):
                 offset = z_n - step + 1 if direction == 0 else step - 1
-                slot = tile_at(half_of(stream_), (depth + offset) % z_n, core)
+                slot = shard_at(half_of(stream_), (depth + offset) % z_n, core)
                 ring_copy(stream_, direction, step, slot).wait_send()
 
 

time: 85 us -> 81.7 us (0.961); the launches traced: 84.7 us -> 80.3 us
  Pallas kernels: 79.7 us -> 75.2 us
    pallas_call x1, Pallas kernels: 79.7 us -> 75.2 us  [per_device(): pl.pallas_call(functools.partial(layer_kernel, cfg), out_shape=(jax.Shape...]
where the time goes in v2:
time: 81.7 us; the launch traced here: 80.3 us
  Pallas kernels  75.2 us (92%)
  local copies, waits for them, and re-layouts  3.15 us (4%)
  between operations  1.94 us (2%)
    pallas_call x1, Pallas kernels, per_device(): pl.pallas_call(functools.partial(layer_kernel, cfg), out_shape=(jax.Shape...  75.2 us
    unnamed x2, local copies, waits for them, and re-layouts  3.15 us

profile of v2, /device:TPU:1, one launch (start us, length us, event | category | flops | bytes accessed | tf_op | source)
XLA Modules:
  0.0 80.3 jit_solution(12655769416306629941)
XLA Ops:
  1.9 75.2 %shard_map.194 = (bf16[3,24,3072]{2,1,0:T(8,128)(2,1)}, f32[2,24,64]{2,1,0:T(8,128)}) custom-call(s32[1]{0:T(128)S(6)} %copy.23.text_len, f32[1]{0:T(128)S(6)} %copy.24.step_size, bf16[3,3,24,3072]{3,2,1,0:T(8,128)(2,1)} %bitcast.15, bf16[3,24,6144]{2,1,0:T(8,128)(2,1)} %bitcast.16, bf16[3,24,3072]{2,1,0:T(8,128)(2,1)} %bitcast.17, ...), custom_call_target="tpu_custom_call" | custom-call | tf_op jit(solution)/shard_map/pallas_call | solution.py:571
  77.1 1.8 %copy.25 = bf16[1,3,24,3072]{3,2,1,0:T(8,128)(2,1)} copy(bf16[1,3,24,3072]{3,2,1,0:T(8,128)(2,1)} %bitcast.18) | data formatting | bytes 884736
  78.9 1.3 %copy.26 = f32[1,2,24,64]{3,2,1,0:T(8,128)} copy(f32[1,2,24,64]{3,2,1,0:T(8,128)} %bitcast.23) | data formatting | bytes 24576

commit v3 on v2

--- a/solution.py
+++ b/solution.py
@@ -76,6 +76,8 @@
     product,
     y_out,
     y_in,
+    y_low,
+    y_sum,
     y_pass,
     y_got,
     x_out,
@@ -99,6 +101,8 @@
     side_recv,
     y_send,
     y_recv,
+    y_low_send,
+    y_low_recv,
     y_pass_send,
     y_pass_recv,
     x_send,
@@ -335,13 +339,27 @@
                 slot = shard_at(half_of(stream_), (depth + offset) % z_n, 1 - core)
                 side_copy(stream_ * z_n + offset, slot, sibling).wait_recv()
 
-    def y_copy(p, dy, peer_y):
-        return pltpu.make_async_remote_copy(
-            src_ref=y_out.at[p, peer_y],
-            dst_ref=y_in.at[p, dy],
-            send_sem=y_send.at[p, dy],
-            recv_sem=y_recv.at[p, dy],
-            device_id={"head": peer_y * 2 + side_x},
+    def first_of(p, y):
+        odd = (p + core) % 2
+        return (1 - odd) * (y + 1 - 2 * (y % 2)) + odd * (y_n - 1 - y)
+
+    def y_copy(p):
+        return pltpu.make_async_remote_copy(
+            src_ref=y_out.at[p],
+            dst_ref=y_in.at[p],
+            send_sem=y_send.at[p],
+            recv_sem=y_recv.at[p],
+            device_id={"head": first_of(p, row_y) * 2 + side_x},
+            device_id_type=MESH,
+        )
+
+    def y_low_copy(p):
+        return pltpu.make_async_remote_copy(
+            src_ref=y_low.at[p],
+            dst_ref=y_sum.at[p],
+            send_sem=y_low_send.at[p],
+            recv_sem=y_low_recv.at[p],
+            device_id={"head": first_of(p + 1, row_y) * 2 + side_x},
             device_id_type=MESH,
         )
 
@@ -381,19 +399,27 @@
     def offset_of(kind, p):
         return p + 1 if kind == 1 else (z_n - p) % z_n
 
-    def pass_on(p):
-        for dy in range(1, y_n):
-            y_copy(p, dy, row_y).wait_recv()
+    def y_second(p):
+        y_copy(p).wait_recv()
+        other = first_of(p + 1, row_y)
+        for side in (0, 1):
+            total = group_rows(0, p, other * 2 + side) + y_in[p, 1, side].astype(F32)
+            y_low[p, side] = total.astype(BF16)
+        y_low_copy(p).start()
+
+    def y_third(p):
+        y_low_copy(p).wait_recv()
         for dx in (0, 1):
             side = (side_x + dx) % 2
             total = group_rows(0, p, row_y * 2 + side)
-            for dy in range(1, y_n):
-                total = total + y_in[p, dy, side].astype(F32)
+            total = total + y_in[p, 0, side].astype(F32) + y_sum[p, side].astype(F32)
             if dx == 0:
                 mine[0, p] = total
             else:
                 y_pass[p] = total.astype(BF16)
         y_pass_copy(p).start()
+
+    def x_second(p):
         x_copy(p).wait_recv()
         for dy in range(1, y_n):
             peer_y = (row_y + dy) % y_n
@@ -405,7 +431,7 @@
     wait_sibling([offset_of(kind, 0) for kind in (0, 1)])
 
     def project(k, _):
-        p, kind = k // 2, k % 2
+        p, kind = k // 2, 1 - k % 2
 
         @pl.when(k == 2)
         def _():
@@ -420,7 +446,7 @@
 
         @pl.when(k == 2 * pairs - 2)
         def _():
-            pass_on(0)
+            y_second(0)
             advance(0, far)
             advance(1, far)
             wait_sibling([offset_of(kind, pairs - 1) for kind in (0, 1)])
@@ -434,11 +460,11 @@
 
         @pl.when(kind == 0)
         def _():
-            for dy in range(1, y_n):
-                peer_y = (row_y + dy) % y_n
+            peer_y = first_of(p, row_y)
+            for place, target in enumerate((peer_y, first_of(p + 1, peer_y))):
                 for side in (0, 1):
-                    y_out[p, peer_y, side] = group_rows(0, p, peer_y * 2 + side).astype(BF16)
-                y_copy(p, dy, peer_y).start()
+                    y_out[p, place, side] = group_rows(0, p, target * 2 + side).astype(BF16)
+            y_copy(p).start()
 
         @pl.when(kind == 1)
         def _():
@@ -459,15 +485,21 @@
             total = total + x_got[p, dy].astype(F32)
         mine[1, p] = total
 
-    def finish(p, _):
-        @pl.when(p < pairs)
-        def _():
-            pass_on(p)
-
-        collect(p - 1)
-        return 0
-
-    lax.fori_loop(1, pairs + 1, finish, 0)
+    x_second(0)
+    y_second(1)
+    y_third(0)
+    y_second(2)
+    x_second(1)
+    y_third(1)
+    y_second(3)
+    x_second(2)
+    y_third(2)
+    y_third(3)
+    x_second(3)
+    collect(0)
+    collect(1)
+    collect(2)
+    collect(3)
 
     def sum_at(z):
         offset = (z + z_n - depth) % z_n
@@ -509,8 +541,9 @@
 
     def drain_parts(p, _):
         for dy in range(1, y_n):
-            y_copy(p, dy, (row_y + dy) % y_n).wait_send()
             x_pass_copy(p, dy).wait_send()
+        y_copy(p).wait_send()
+        y_low_copy(p).wait_send()
         y_pass_copy(p).wait_send()
         x_copy(p).wait_send()
         return 0
@@ -586,8 +619,10 @@
                 pltpu.VMEM((rows, units), F32),
                 pltpu.VMEM((rows, width + units), BF16),
                 pltpu.VMEM((2, pairs, rows, columns), F32),
-                pltpu.VMEM((pairs, y_n, 2, own_rows, columns), BF16),
-                pltpu.VMEM((pairs, y_n, 2, own_rows, columns), BF16),
+                pltpu.VMEM((pairs, 2, 2, own_rows, columns), BF16),
+                pltpu.VMEM((pairs, 2, 2, own_rows, columns), BF16),
+                pltpu.VMEM((pairs, 2, own_rows, columns), BF16),
+                pltpu.VMEM((pairs, 2, own_rows, columns), BF16),
                 pltpu.VMEM((pairs, own_rows, columns), BF16),
                 pltpu.VMEM((pairs, own_rows, columns), BF16),
                 pltpu.VMEM((pairs, y_n, own_rows, columns), BF16),
@@ -609,8 +644,10 @@
                 dma((2, 2, z_n)),
                 dma((2 * z_n + 1,)),
                 dma((2 * z_n + 1,)),
-                dma((pairs, y_n)),
-                dma((pairs, y_n)),
+                dma((pairs,)),
+                dma((pairs,)),
+                dma((pairs,)),
+                dma((pairs,)),
                 dma((pairs,)),
                 dma((pairs,)),
                 dma((pairs,)),

time: 81.7 us -> 80.2 us (0.982); the launches traced: 80.3 us -> 80 us
  no operation moved by 1% of the time
where the time goes in v3:
time: 80.2 us; the launch traced here: 80 us
  Pallas kernels  74.9 us (93%)
  local copies, waits for them, and re-layouts  3.15 us (4%)
  between operations  1.94 us (2%)
    pallas_call x1, Pallas kernels, per_device(): pl.pallas_call(functools.partial(layer_kernel, cfg), out_shape=(jax.Shape...  74.9 us
    unnamed x2, local copies, waits for them, and re-layouts  3.15 us

profile of v3, /device:TPU:1, one launch (start us, length us, event | category | flops | bytes accessed | tf_op | source)
XLA Modules:
  0.0 80.0 jit_solution(5647247651882391270)
XLA Ops:
  1.9 74.9 %shard_map.194 = (bf16[3,24,3072]{2,1,0:T(8,128)(2,1)}, f32[2,24,64]{2,1,0:T(8,128)}) custom-call(s32[1]{0:T(128)S(6)} %copy.23.text_len, f32[1]{0:T(128)S(6)} %copy.24.step_size, bf16[3,3,24,3072]{3,2,1,0:T(8,128)(2,1)} %bitcast.15, bf16[3,24,6144]{2,1,0:T(8,128)(2,1)} %bitcast.16, bf16[3,24,3072]{2,1,0:T(8,128)(2,1)} %bitcast.17, ...), custom_call_target="tpu_custom_call" | custom-call | tf_op jit(solution)/shard_map/pallas_call | solution.py:604
  76.8 1.8 %copy.25 = bf16[1,3,24,3072]{3,2,1,0:T(8,128)(2,1)} copy(bf16[1,3,24,3072]{3,2,1,0:T(8,128)(2,1)} %bitcast.18) | data formatting | bytes 884736
  78.6 1.3 %copy.26 = f32[1,2,24,64]{3,2,1,0:T(8,128)} copy(f32[1,2,24,64]{3,2,1,0:T(8,128)} %bitcast.23) | data formatting | bytes 24576

commit v4 on v3

--- a/solution.py
+++ b/solution.py
@@ -559,6 +559,11 @@
                 offset = z_n - step + 1 if direction == 0 else step - 1
                 slot = shard_at(half_of(stream_), (depth + offset) % z_n, core)
                 ring_copy(stream_, direction, step, slot).wait_send()
+
+
+def hand_on(hidden_in, latent_in, hidden_out, latent_out):
+    hidden_out[...] = hidden_in[...]
+    latent_out[...] = latent_in[...]
 
 
 def solution(mesh):
@@ -679,6 +684,15 @@
             b_final[None],
             latent[0],
         )
+        hidden, latent_next = pl.pallas_call(
+            hand_on,
+            out_shape=(
+                jax.ShapeDtypeStruct(hidden.shape, hidden.dtype),
+                jax.ShapeDtypeStruct(latent_next.shape, latent_next.dtype),
+            ),
+            in_specs=[vmem, vmem],
+            out_specs=(vmem, vmem),
+        )(hidden, latent_next)
         return hidden[None], latent_next[None]
 
     placed = (

time: 80.2 us -> 78.8 us (0.983)
  local copies, waits for them, and re-layouts: 3.15 us -> 0 us
  Pallas kernels: 74.9 us -> 76.7 us
    unnamed x2 -> x0, local copies, waits for them, and re-layouts: 3.15 us -> none
    pallas_call x0 -> x1, Pallas kernels: none -> 1.81 us  [per_device(): pl.pallas_call(hand_on, out_shape=(jax.ShapeDtypeStruct(hidden.shape, hid...]
where the time goes in v4:
time: 78.8 us; the launch traced here: 78.6 us
  Pallas kernels  76.7 us (97%)
  between operations  1.94 us (2%)
    pallas_call x1, Pallas kernels, per_device(): pl.pallas_call(functools.partial(layer_kernel, cfg), out_shape=(jax.Shape...  74.9 us
    pallas_call x1, Pallas kernels, per_device(): pl.pallas_call(hand_on, out_shape=(jax.ShapeDtypeStruct(hidden.shape, hid...  1.81 us

profile of v4, /device:TPU:1, one launch (start us, length us, event | category | flops | bytes accessed | tf_op | source)
XLA Modules:
  0.0 78.6 jit_solution(18171479538746041944)
XLA Ops:
  1.9 74.9 %shard_map.194 = (bf16[3,24,3072]{2,1,0:T(8,128)(2,1)}, f32[2,24,64]{2,1,0:T(8,128)}) custom-call(s32[1]{0:T(128)S(6)} %copy.21.text_len, f32[1]{0:T(128)S(6)} %copy.22.step_size, bf16[3,3,24,3072]{3,2,1,0:T(8,128)(2,1)} %bitcast.15, bf16[3,24,6144]{2,1,0:T(8,128)(2,1)} %bitcast.16, bf16[3,24,3072]{2,1,0:T(8,128)(2,1)} %bitcast.17, ...), custom_call_target="tpu_custom_call" | custom-call | tf_op jit(solution)/shard_map/pallas_call | solution.py:609
  76.8 1.8 %shard_map.195 = (bf16[3,24,3072]{2,1,0:T(8,128)(2,1)}, f32[2,24,64]{2,1,0:T(8,128)}) custom-call(bf16[3,24,3072]{2,1,0:T(8,128)(2,1)} %get-tuple-element.6.hidden_in, f32[2,24,64]{2,1,0:T(8,128)} %get-tuple-element.7.latent_in), custom_call_target="tpu_custom_call" | custom-call | tf_op jit(solution)/shard_map/pallas_call | solution.py:687

commit v5 on v4

--- a/solution.py
+++ b/solution.py
@@ -561,9 +561,15 @@
                 ring_copy(stream_, direction, step, slot).wait_send()
 
 
-def hand_on(hidden_in, latent_in, hidden_out, latent_out):
-    hidden_out[...] = hidden_in[...]
-    latent_out[...] = latent_in[...]
+def hand_on(hidden_in, latent_in, hidden_out, latent_out, sem):
+    copies = (
+        pltpu.make_async_copy(hidden_in, hidden_out, sem.at[0]),
+        pltpu.make_async_copy(latent_in, latent_out, sem.at[1]),
+    )
+    for copy in copies:
+        copy.start()
+    for copy in copies:
+        copy.wait()
 
 
 def solution(mesh):
@@ -691,7 +697,8 @@
                 jax.ShapeDtypeStruct(latent_next.shape, latent_next.dtype),
             ),
             in_specs=[vmem, vmem],
-            out_specs=(vmem, vmem),
+            out_specs=(any_, any_),
+            scratch_shapes=[dma((2,))],
         )(hidden, latent_next)
         return hidden[None], latent_next[None]
 

time: 78.8 us -> 78.8 us (level)
  no operation moved by 1% of the time
where the time goes in v5:
time: 78.8 us; the launch traced here: 78.6 us
  Pallas kernels  76.7 us (97%)
  between operations  1.94 us (2%)
    pallas_call x1, Pallas kernels, per_device(): pl.pallas_call(functools.partial(layer_kernel, cfg), out_shape=(jax.Shape...  74.9 us
    pallas_call x1, Pallas kernels, per_device(): pl.pallas_call(hand_on, out_shape=(jax.ShapeDtypeStruct(hidden.shape, hid...  1.8 us

profile of v5, /device:TPU:1, one launch (start us, length us, event | category | flops | bytes accessed | tf_op | source)
XLA Modules:
  0.0 78.6 jit_solution(12895910093596627998)
XLA Ops:
  1.9 74.9 %shard_map.194 = (bf16[3,24,3072]{2,1,0:T(8,128)(2,1)}, f32[2,24,64]{2,1,0:T(8,128)}) custom-call(s32[1]{0:T(128)S(6)} %copy.21.text_len, f32[1]{0:T(128)S(6)} %copy.22.step_size, bf16[3,3,24,3072]{3,2,1,0:T(8,128)(2,1)} %bitcast.15, bf16[3,24,6144]{2,1,0:T(8,128)(2,1)} %bitcast.16, bf16[3,24,3072]{2,1,0:T(8,128)(2,1)} %bitcast.17, ...), custom_call_target="tpu_custom_call" | custom-call | tf_op jit(solution)/shard_map/pallas_call | solution.py:615
  76.8 1.8 %shard_map.195 = (bf16[3,24,3072]{2,1,0:T(8,128)(2,1)}, f32[2,24,64]{2,1,0:T(8,128)}) custom-call(bf16[3,24,3072]{2,1,0:T(8,128)(2,1)} %get-tuple-element.6.hidden_in, f32[2,24,64]{2,1,0:T(8,128)} %get-tuple-element.7.latent_in), custom_call_target="tpu_custom_call" | custom-call | tf_op jit(solution)/shard_map/pallas_call | solution.py:693
